TPU v7x, 512 devices: a whole 4x4x16 slice. The times are simulated.
512 devices in a mesh: leaf: 32 (over x, y, core), blk: 16 (over z).
Axes of the slice: x: 4, y: 4, z: 16, core: 2. Of those that a mesh axis runs over, the one named last changes fastest.
Arguments:
- points: float32 [3, 131072], P(None, ('leaf', 'blk')), may hold values from 0 to 1
- iterate: bfloat16 [131072, 256], P(('leaf', 'blk')), may hold values from -6 to 6
- right_side: float32 [131072, 256], P(('leaf', 'blk')), may hold values from -6 to 6
- near_mask: int32 [512, 16], P(('leaf', 'blk')), may hold values from 0 to 1, as said below
- leaf_inverse: bfloat16 [512, 256, 256], P(('leaf', 'blk'))
- skeleton: int32 [3, 32, 512], P(None, 'leaf'), may hold values from 0 to 4095, as said below
- coupling: bfloat16 [3, 32, 512, 512], P(None, 'leaf'), may hold values from -0.25 to 0.25
- reduced_inverse: bfloat16 [3, 32, 512, 512], P(None, 'leaf')
- lift: bfloat16 [3, 131072, 512], P(None, ('leaf', 'blk')), may hold values from -0.25 to 0.25
Outputs:
- correction: float32 [131072, 256], P(('leaf', 'blk'))
Inputs may be any that keep to these rules, and one draw needn't show every extreme that they name: near_mask[i, i mod 16] is 1. `skeleton`: the 512 indices of one level and subtree are distinct.
All inputs are finite; a program needn't handle non-finite values.
Results may differ from a plain program's by a relative error of at most 0.014.
Values may be sent and summed in bfloat16 or wider, within the bound.
No kernel may reach another device: no remote copies, remote signals or barrier semaphores. Data moves between devices by JAX's collectives and lax.ppermute only.
A program may use at most 64 MiB of HBM per device.

v0:
```python
import jax
import jax.numpy as jnp
from jax import lax
from jax.sharding import PartitionSpec as P

LEVELS = 3
kernel_scale = 0.125
spread_coef = 4.0
shift_value = 1.0


def from_partner(block, axis, distance):
    count = lax.axis_size(axis)
    route = []
    for low in range(count):
        high = low | 1 << distance
        if high != low and high < count:
            route += [(low, high), (high, low)]
    return lax.ppermute(block, axis, route)


def kernel_block(left, right):
    dist = jnp.zeros((left.shape[1], right.shape[1]), jnp.float32)
    for axis_no in range(3):
        diff = left[axis_no][:, None] - right[axis_no][None, :]
        dist = dist + diff * diff
    return kernel_scale * jnp.exp(-spread_coef * dist)


def sibling_solve(cpl, inverse, part_total, level_no):
    own_total = part_total
    for bit_no in range(level_no):
        own_total = own_total + from_partner(own_total, "leaf", bit_no)
    other_total = from_partner(own_total.astype(jnp.bfloat16), "leaf", level_no).astype(
        own_total.dtype
    )
    rhs = own_total - jnp.dot(
        cpl, other_total.astype(jnp.bfloat16), preferred_element_type=jnp.float32
    )
    return jnp.dot(inverse, rhs.astype(jnp.bfloat16), preferred_element_type=jnp.float32)


def on_device(
    points, iterate, right_side, near_mask, leaf_inverse, skeleton, coupling, reduced_inverse, lift
):
    tile_rows = points.shape[1]
    all_pts = lax.all_gather(points, "blk", axis=1, tiled=True)
    mask_row = near_mask[0].astype(jnp.bfloat16)
    block_rows = lax.all_gather(iterate, "blk", axis=0, tiled=True)
    count = block_rows.shape[0]
    col_block = jnp.arange(count, dtype=jnp.int32) // tile_rows
    col_mask = jnp.take(mask_row, col_block)
    kernel = kernel_block(points, all_pts).astype(jnp.bfloat16)
    near = jnp.dot(kernel * col_mask[None, :], block_rows, preferred_element_type=jnp.float32)
    resid = right_side - shift_value * iterate.astype(jnp.float32) - near
    field = jnp.dot(leaf_inverse[0], resid.astype(jnp.bfloat16), preferred_element_type=jnp.float32)
    blk_start = lax.axis_index("blk") * tile_rows
    for level_no in range(LEVELS):
        local_index = skeleton[level_no, 0] - blk_start
        inside = (local_index >= 0) & (local_index < tile_rows)
        rows_taken = jnp.take(field, jnp.clip(local_index, 0, tile_rows - 1), axis=0)
        picked = jnp.where(inside[:, None], rows_taken, 0.0)
        part_total = lax.psum(picked, "blk")
        answer = sibling_solve(
            coupling[level_no, 0], reduced_inverse[level_no, 0], part_total, level_no
        ).astype(jnp.bfloat16)
        field = field - jnp.dot(lift[level_no], answer, preferred_element_type=jnp.float32)
    return field


def solution(mesh):
    in_specs = (
        P(None, ("leaf", "blk")),
        P(("leaf", "blk"), None),
        P(("leaf", "blk"), None),
        P(("leaf", "blk"), None),
        P(("leaf", "blk"), None, None),
        P(None, "leaf", None),
        P(None, "leaf", None, None),
        P(None, "leaf", None, None),
        P(None, ("leaf", "blk"), None),
    )
    out_specs = P(("leaf", "blk"), None)
    return jax.shard_map(
        on_device, mesh=mesh, in_specs=in_specs, out_specs=out_specs, check_vma=False
    )
```

profile of v0, /device:TPU:2, one launch (start us, length us, event | category | flops | bytes accessed | tf_op | source)
XLA Modules:
  0.0 568.9 jit_solution(15477949225896639626)
XLA Ops:
  6.5 0.7 all-gather.2.cloned.1.call-update
  7.3 0.7 convert_element_type.53
  8.1 0.1 compare_reduce_fusion.3
  8.4 0.1 compare_reduce_fusion.7
  8.5 36.0 %all_gather.6 = f32[3,4096]{1,0:T(4,128)S(1)} all-gather(f32[3,256]{1,0:T(4,128)} %param.11), channel_id=1, replica_groups=mesh['leaf'=32,'blk'=16] {'blk'}, dimensions={1}, use_global_device_ids=true | all-gather | bytes 52224 | tf_op jit(solution)/shard_map/all_gather | solution.py:47
  44.5 0.7 fusion.79
  45.2 4.3 fusion.67
  49.5 0.7 broadcast_clamp_fusion
  50.2 0.8 and_reduce_fusion
  51.0 0.8 fusion.78
  51.8 5.7 %fusion.69 = bf16[4096]{0:T(1024)(128)(2,1)S(1)} fusion(pred[4096]{0:T(1024)(128)(4,1)S(1)} %compare_reduce_fusion, pred[4096]{0:T(1024)(128)(4,1)S(1)} %compare_reduce_fusion.1, pred[4096]{0:T(1024)(128)(4,1)S(1)} %compare_reduce_fusion.2, pred[4096]{0:T(1024)(128)(4,1)S(1)} %compare_reduce_fusion.3, pred[4096]{0:T(1024)(128)(4,1)S(1)} %compare_reduce_fusion.4, ...), kind=kLoop, calls=%fused_computation.94 | loop fusion | flops 98304 | bytes 53266 | tf_op jit(solution)/shard_map/jit(_take)/select_n | solution.py:52
  57.6 29.0 %all-gather.2.cloned.1.call-done = bf16[4096,256]{1,0:T(8,128)(2,1)} async-done(((bf16[256,256]{1,0:T(8,128)(2,1)}), bf16[4096,256]{1,0:T(8,128)(2,1)}) %all-gather.2.cloned.1.call-update) | async-done | bytes 2097168 | tf_op jit(solution)/shard_map/all_gather | solution.py:49
  86.6 3.9 convolution_bitcast_fusion.3
  90.5 0.1 copy.14
  90.7 1.6 gather_fusion
  92.3 1.0 select_select_fusion.2
  93.4 135.0 %all-reduce.4.cloned.1.call-done = f32[512,256]{1,0:T(8,128)} async-done(((f32[512,256]{1,0:T(8,128)}), f32[512,256]{1,0:T(8,128)}) %all-reduce.4.cloned.1.call-update) | async-done | bytes 524304 | tf_op jit(solution)/shard_map/psum | solution.py:63
  228.4 1.1 convert_element_type.56
  229.4 1.9 collective-permute-start
  231.4 1.5 collective-permute-done
  232.9 1.3 fusion.16
  234.2 1.6 fusion.25
  235.8 0.1 copy.15
  236.0 1.6 gather_fusion.1
  237.6 1.0 select_select_fusion.1
  238.7 134.5 %all-reduce.6.cloned.1.call-done = f32[512,256]{1,0:T(8,128)} async-done(((f32[512,256]{1,0:T(8,128)}), f32[512,256]{1,0:T(8,128)}) %all-reduce.6.cloned.1.call-update) | async-done | bytes 524304 | tf_op jit(solution)/shard_map/psum | solution.py:63
  373.2 1.9 collective-permute-start.1
  375.1 2.1 collective-permute-done.1
  377.2 1.1 fusion.76
  378.3 3.4 collective-permute-start.2
  381.7 6.8 %collective-permute-done.2 = bf16[512,256]{1,0:T(8,128)(2,1)S(1)} collective-permute-done((bf16[512,256]{1,0:T(8,128)(2,1)S(1)}, bf16[512,256]{1,0:T(8,128)(2,1)S(1)}, u32[]{:S(2)}, u32[]{:S(2)}) %collective-permute-start.2) | collective-permute-done | bytes 262176 | tf_op jit(solution)/shard_map/ppermute | solution.py:19
  388.5 0.3 fusion.15
  388.8 1.6 fusion.24
  390.4 0.1 copy.16
  390.5 1.6 gather_fusion.2
  392.1 1.0 select_select_fusion
  393.2 134.6 %all-reduce.8.cloned.1.call-done = f32[512,256]{1,0:T(8,128)} async-done(((f32[512,256]{1,0:T(8,128)}), f32[512,256]{1,0:T(8,128)}) %all-reduce.8.cloned.1.call-update) | async-done | bytes 524304 | tf_op jit(solution)/shard_map/psum | solution.py:63
  527.8 1.9 collective-permute-start.3
  529.7 2.1 collective-permute-done.3
  531.8 1.1 add.73
  532.9 3.4 collective-permute-start.4
  536.3 12.5 %collective-permute-done.4 = f32[512,256]{1,0:T(8,128)S(1)} collective-permute-done((f32[512,256]{1,0:T(8,128)S(1)}, f32[512,256]{1,0:T(8,128)S(1)}, u32[]{:S(2)}, u32[]{:S(2)}) %collective-permute-start.4) | collective-permute-done | bytes 524320 | tf_op jit(solution)/shard_map/ppermute | solution.py:19
  548.7 0.1 fusion.75
  548.8 4.9 collective-permute-start.5
  553.7 6.0 %collective-permute-done.5 = bf16[512,256]{1,0:T(8,128)(2,1)S(1)} collective-permute-done((bf16[512,256]{1,0:T(8,128)(2,1)S(1)}, bf16[512,256]{1,0:T(8,128)(2,1)S(1)}, u32[]{:S(2)}, u32[]{:S(2)}) %collective-permute-start.5) | collective-permute-done | bytes 262176 | tf_op jit(solution)/shard_map/ppermute | solution.py:19
  559.7 0.3 fusion.14
  560.0 1.6 fusion.23
  561.6 0.8 copy.17
  (30 shorter events, 0.7 us)
Async XLA Ops:
  6.5 80.1 %copy-start = (bf16[1,256,256]{2,1,0:T(8,128)(2,1)S(1)}, bf16[1,256,256]{2,1,0:T(8,128)(2,1)}, u32[]{:S(2)}) copy-start(bf16[1,256,256]{2,1,0:T(8,128)(2,1)} %param.15) | copy-start | bytes 393220
  6.5 80.1 %all-gather.2.cloned.1.call-start = ((), (), s32[]{:S(2)}) async-start(), calls=%async_computation | async-start | bytes 2228224 | tf_op jit(solution)/shard_map/all_gather | solution.py:49
  7.3 221.1 %all-reduce.4.cloned.1.call-start = ((), (), s32[]{:S(2)}) async-start(), calls=%async_computation.1 | async-start | bytes 1048576 | tf_op jit(solution)/shard_map/psum | solution.py:63
  92.3 140.6 %copy-start.1 = (bf16[3,1,512,512]{3,2,1,0:T(8,128)(2,1)S(1)}, bf16[3,1,512,512]{3,2,1,0:T(8,128)(2,1)}, u32[]{:S(2)}) copy-start(bf16[3,1,512,512]{3,2,1,0:T(8,128)(2,1)} %param.17) | copy-start | bytes 4718596
  93.3 279.9 %all-reduce.6.cloned.1.call-start = ((), (), s32[]{:S(2)}) async-start(), calls=%async_computation.2 | async-start | bytes 1048576 | tf_op jit(solution)/shard_map/psum | solution.py:63
  229.4 3.4 collective-permute-start
  238.6 150.2 %copy-start.2 = (bf16[3,256,512]{2,1,0:T(8,128)(2,1)S(1)}, bf16[3,256,512]{2,1,0:T(8,128)(2,1)}, u32[]{:S(2)}) copy-start(bf16[3,256,512]{2,1,0:T(8,128)(2,1)} %param.19) | copy-start | bytes 2359300
  238.6 289.2 %all-reduce.8.cloned.1.call-start = ((), (), s32[]{:S(2)}) async-start(), calls=%async_computation.3 | async-start | bytes 1048576 | tf_op jit(solution)/shard_map/psum | solution.py:63
  373.2 4.0 collective-permute-start.1
  378.3 10.2 %collective-permute-start.2 = (bf16[512,256]{1,0:T(8,128)(2,1)S(1)}, bf16[512,256]{1,0:T(8,128)(2,1)S(1)}, u32[]{:S(2)}, u32[]{:S(2)}) collective-permute-start(bf16[512,256]{1,0:T(8,128)(2,1)S(1)} %get-tuple-element.11), channel_id=1, source_target_pairs={{0,32},{32,0},{16,48},{48,16},{64,96},{96,64},{80,112},{112,80},{1... | collective-permute-start | bytes 786440 | tf_op jit(solution)/shard_map/ppermute | solution.py:19
  527.8 4.0 collective-permute-start.3
  532.9 15.9 %collective-permute-start.4 = (f32[512,256]{1,0:T(8,128)S(1)}, f32[512,256]{1,0:T(8,128)S(1)}, u32[]{:S(2)}, u32[]{:S(2)}) collective-permute-start(f32[512,256]{1,0:T(8,128)S(1)} %add.73), channel_id=1, source_target_pairs={{0,32},{32,0},{16,48},{48,16},{64,96},{96,64},{80,112},{112,80},{1... | collective-permute-start | bytes 1572872 | tf_op jit(solution)/shard_map/ppermute | solution.py:19
  548.8 10.9 %collective-permute-start.5 = (bf16[512,256]{1,0:T(8,128)(2,1)S(1)}, bf16[512,256]{1,0:T(8,128)(2,1)S(1)}, u32[]{:S(2)}, u32[]{:S(2)}) collective-permute-start(bf16[512,256]{1,0:T(8,128)(2,1)S(1)} %get-tuple-element.9), channel_id=1, source_target_pairs={{0,64},{64,0},{16,80},{80,16},{32,96},{96,32},{48,112},{112,48},{1... | collective-permute-start | bytes 786440 | tf_op jit(solution)/shard_map/ppermute | solution.py:19
Sparse Core Ops, SparseCore 0:
  9.4 77.1 all-gather.1
  93.4 134.8 all-reduce.3
  238.7 134.3 all-reduce.5
  393.3 134.4 all-reduce.7
where the time goes:
time: 570 us; the launch traced here: 569 us
  waiting for transfers between devices  465 us (82%)
  blocking collectives  36 us (6%)
  other arithmetic  19.1 us (3%)
  starting transfers between devices  17.6 us (3%)
  between operations  13.4 us (2%)
  matrix products  10.6 us (2%)
  local copies, waits for them, and re-layouts  7.5 us (1%)
    psum x3, waiting for transfers between devices, on_device(): part_total = lax.psum(picked, 'blk')  404 us
    all_gather x1, blocking collectives, on_device(): all_pts = lax.all_gather(points, 'blk', axis=1, tiled=True)  36 us
    ppermute x6, waiting for transfers between devices, from_partner(): return lax.ppermute(block, axis, route)  30.9 us
    all_gather x1, waiting for transfers between devices, on_device(): block_rows = lax.all_gather(iterate, 'blk', axis=0, tiled=True)  29 us
    ppermute x6, starting transfers between devices, from_partner(): return lax.ppermute(block, axis, route)  17.4 us
  transfers between devices with their start and end apart: 10, of which 10 were waited for; matrix products, arithmetic and copies ran while one was open for 3% of the time, Pallas kernels for 0%

commit v1 on v0

--- a/solution.py
+++ b/solution.py
@@ -46,7 +46,9 @@
     tile_rows = points.shape[1]
     all_pts = lax.all_gather(points, "blk", axis=1, tiled=True)
     mask_row = near_mask[0].astype(jnp.bfloat16)
-    block_rows = lax.all_gather(iterate, "blk", axis=0, tiled=True)
+    block_rows = jnp.concatenate(
+        lax.all_to_all(jnp.stack([iterate] * lax.axis_size("blk")), "blk", 0, 0), axis=0
+    )
     count = block_rows.shape[0]
     col_block = jnp.arange(count, dtype=jnp.int32) // tile_rows
     col_mask = jnp.take(mask_row, col_block)

time: 570 us -> 635 us (1.11)
  blocking collectives: 36 us -> 116 us
  waiting for transfers between devices: 465 us -> 437 us
  starting transfers between devices: 17.6 us -> 32.9 us
    all_gather x1, blocking collectives: 36 us -> 116 us  [on_device(): all_pts = lax.all_gather(points, 'blk', axis=1, tiled=True)]
    all_gather x1 -> x0, waiting for transfers between devices: 29 us -> none  [on_device(): block_rows = lax.all_gather(iterate, 'blk', axis=0, tiled=True)]
    all_to_all x0 -> x1, starting transfers between devices: none -> 15.3 us  [on_device(): lax.all_to_all(jnp.stack([iterate] * lax.axis_size('blk')), 'blk', 0, 0)]
  transfers between devices with their start and end apart: 10 -> 10, of which waited for: 10 -> 9; matrix products, arithmetic and copies ran while one was open for 3% -> 2% of each run, Pallas kernels for 0% -> 0%
where the time goes in v1:
time: 635 us; the launch traced here: 634 us
  waiting for transfers between devices  437 us (69%)
  blocking collectives  116 us (18%)
  starting transfers between devices  32.9 us (5%)
  other arithmetic  17.1 us (3%)
  between operations  13.5 us (2%)
  local copies, waits for them, and re-layouts  9.21 us (1%)
  matrix products  9.06 us (1%)
    psum x3, waiting for transfers between devices, on_device(): part_total = lax.psum(picked, 'blk')  406 us
    all_gather x1, blocking collectives, on_device(): all_pts = lax.all_gather(points, 'blk', axis=1, tiled=True)  116 us
    ppermute x6, waiting for transfers between devices, from_partner(): return lax.ppermute(block, axis, route)  30.9 us
    ppermute x6, starting transfers between devices, from_partner(): return lax.ppermute(block, axis, route)  17.4 us
    all_to_all x1, starting transfers between devices, on_device(): lax.all_to_all(jnp.stack([iterate] * lax.axis_size('blk')), 'blk', 0, 0)  15.3 us
  transfers between devices with their start and end apart: 10, of which 9 were waited for; matrix products, arithmetic and copies ran while one was open for 2% of the time, Pallas kernels for 0%

profile of v1, /device:TPU:2, one launch (start us, length us, event | category | flops | bytes accessed | tf_op | source)
XLA Modules:
  0.0 634.5 jit_solution(17288810654655032047)
XLA Ops:
  6.5 2.5 stack.2
  9.1 15.3 %all-to-all-start = ((bf16[16,256,256]{2,1,0:T(8,128)(2,1)}), bf16[16,256,256]{2,1,0:T(8,128)(2,1)S(1)}, u32[]{:S(2)}, u32[]{:S(2)}) async-start(bf16[16,256,256]{2,1,0:T(8,128)(2,1)} %stack.2), calls=%async_computation | async-start | bytes 4194304 | tf_op jit(solution)/shard_map/all_to_all | solution.py:50
  24.5 0.1 compare_reduce_fusion
  24.5 0.1 compare_reduce_fusion.1
  24.6 0.1 compare_reduce_fusion.2
  24.7 0.1 compare_reduce_fusion.3
  24.9 0.1 compare_reduce_fusion.7
  25.0 0.1 compare_reduce_fusion.8
  25.0 115.7 %all_gather.3 = f32[3,4096]{1,0:T(4,128)S(1)} all-gather(f32[3,256]{1,0:T(4,128)S(1)} %copy-done.4), channel_id=1, replica_groups=mesh['leaf'=32,'blk'=16] {'blk'}, dimensions={1}, use_global_device_ids=true | all-gather | bytes 52224 | tf_op jit(solution)/shard_map/all_gather | solution.py:47
  140.8 0.7 fusion.79
  141.5 4.3 fusion.67
  145.9 5.7 fusion.69
  151.7 2.2 convolution_bitcast_fusion.3
  154.0 0.1 copy.14
  154.1 1.6 gather_fusion
  155.7 1.0 select_select_fusion.2
  156.8 137.0 %all-reduce.4.cloned.1.call-done = f32[512,256]{1,0:T(8,128)} async-done(((f32[512,256]{1,0:T(8,128)}), f32[512,256]{1,0:T(8,128)}) %all-reduce.4.cloned.1.call-update) | async-done | bytes 524304 | tf_op jit(solution)/shard_map/psum | solution.py:65
  293.8 1.1 convert_element_type.56
  294.8 1.9 collective-permute-start
  296.8 1.5 collective-permute-done
  298.3 1.3 fusion.16
  299.6 1.6 fusion.25
  301.3 0.1 copy.15
  301.4 1.6 gather_fusion.1
  303.0 1.0 select_select_fusion.1
  304.1 134.5 %all-reduce.6.cloned.1.call-done = f32[512,256]{1,0:T(8,128)} async-done(((f32[512,256]{1,0:T(8,128)}), f32[512,256]{1,0:T(8,128)}) %all-reduce.6.cloned.1.call-update) | async-done | bytes 524304 | tf_op jit(solution)/shard_map/psum | solution.py:65
  438.6 1.9 collective-permute-start.1
  440.5 2.1 collective-permute-done.1
  442.6 1.2 fusion.76
  443.7 3.4 collective-permute-start.2
  447.2 6.8 %collective-permute-done.2 = bf16[512,256]{1,0:T(8,128)(2,1)S(1)} collective-permute-done((bf16[512,256]{1,0:T(8,128)(2,1)S(1)}, bf16[512,256]{1,0:T(8,128)(2,1)S(1)}, u32[]{:S(2)}, u32[]{:S(2)}) %collective-permute-start.2) | collective-permute-done | bytes 262176 | tf_op jit(solution)/shard_map/ppermute | solution.py:19
  454.0 0.3 fusion.15
  454.3 1.6 fusion.24
  455.9 0.1 copy.16
  456.1 1.6 gather_fusion.2
  457.6 1.0 select_select_fusion
  458.7 134.5 %all-reduce.8.cloned.1.call-done = f32[512,256]{1,0:T(8,128)} async-done(((f32[512,256]{1,0:T(8,128)}), f32[512,256]{1,0:T(8,128)}) %all-reduce.8.cloned.1.call-update) | async-done | bytes 524304 | tf_op jit(solution)/shard_map/psum | solution.py:65
  593.2 1.9 collective-permute-start.3
  595.1 2.1 collective-permute-done.3
  597.2 1.1 add.73
  598.3 3.4 collective-permute-start.4
  601.7 12.5 %collective-permute-done.4 = f32[512,256]{1,0:T(8,128)S(1)} collective-permute-done((f32[512,256]{1,0:T(8,128)S(1)}, f32[512,256]{1,0:T(8,128)S(1)}, u32[]{:S(2)}, u32[]{:S(2)}) %collective-permute-start.4) | collective-permute-done | bytes 524320 | tf_op jit(solution)/shard_map/ppermute | solution.py:19
  614.2 0.1 fusion.75
  614.3 4.9 collective-permute-start.5
  619.2 6.0 collective-permute-done.5
  625.1 0.3 fusion.14
  625.5 1.6 fusion.23
  627.1 0.8 copy.17
  (38 shorter events, 0.5 us)
Async XLA Ops:
  6.5 145.1 %copy-start = (bf16[1,256,256]{2,1,0:T(8,128)(2,1)S(1)}, bf16[1,256,256]{2,1,0:T(8,128)(2,1)}, u32[]{:S(2)}) copy-start(bf16[1,256,256]{2,1,0:T(8,128)(2,1)} %param.15) | copy-start | bytes 393220
  9.0 15.4 %copy-start.6 = (s32[1,16]{1,0:T(1,128)S(1)}, s32[1,16]{1,0:T(1,128)}, u32[]{:S(2)}) copy-start(s32[1,16]{1,0:T(1,128)} %param.14) | copy-start | bytes 196
  9.0 16.0 %copy-start.4 = (f32[3,256]{1,0:T(4,128)S(1)}, f32[3,256]{1,0:T(4,128)}, u32[]{:S(2)}) copy-start(f32[3,256]{1,0:T(4,128)} %param.11) | copy-start | bytes 9220
  9.0 136.7 %copy-start.3 = (s32[3,1,512]{2,1,0:T(1,128)S(1)}, s32[3,1,512]{2,1,0:T(1,128)}, u32[]{:S(2)}) copy-start(s32[3,1,512]{2,1,0:T(1,128)} %param.16) | copy-start | bytes 18436
  9.0 142.7 %copy-start.2 = (bf16[256,256]{1,0:T(8,128)(2,1)S(1)}, bf16[256,256]{1,0:T(8,128)(2,1)}, u32[]{:S(2)}) copy-start(bf16[256,256]{1,0:T(8,128)(2,1)} %param.12) | copy-start | bytes 393220
  9.0 142.7 %copy-start.5 = (f32[256,256]{1,0:T(8,128)S(1)}, f32[256,256]{1,0:T(8,128)}, u32[]{:S(2)}) copy-start(f32[256,256]{1,0:T(8,128)} %param.13) | copy-start | bytes 786436
  9.1 142.6 %all-to-all-start = ((bf16[16,256,256]{2,1,0:T(8,128)(2,1)}), bf16[16,256,256]{2,1,0:T(8,128)(2,1)S(1)}, u32[]{:S(2)}, u32[]{:S(2)}) async-start(bf16[16,256,256]{2,1,0:T(8,128)(2,1)} %stack.2), calls=%async_computation | async-start | bytes 4194304 | tf_op jit(solution)/shard_map/all_to_all | solution.py:50
  24.4 269.4 %all-reduce.4.cloned.1.call-start = ((), (), s32[]{:S(2)}) async-start(), calls=%async_computation.1 | async-start | bytes 1048576 | tf_op jit(solution)/shard_map/psum | solution.py:65
  155.7 142.6 %copy-start.1 = (bf16[3,1,512,512]{3,2,1,0:T(8,128)(2,1)S(1)}, bf16[3,1,512,512]{3,2,1,0:T(8,128)(2,1)}, u32[]{:S(2)}) copy-start(bf16[3,1,512,512]{3,2,1,0:T(8,128)(2,1)} %param.17) | copy-start | bytes 4718596
  156.7 281.8 %all-reduce.6.cloned.1.call-start = ((), (), s32[]{:S(2)}) async-start(), calls=%async_computation.2 | async-start | bytes 1048576 | tf_op jit(solution)/shard_map/psum | solution.py:65
  294.8 3.4 collective-permute-start
  304.0 289.2 %all-reduce.8.cloned.1.call-start = ((), (), s32[]{:S(2)}) async-start(), calls=%async_computation.3 | async-start | bytes 1048576 | tf_op jit(solution)/shard_map/psum | solution.py:65
  438.6 4.0 collective-permute-start.1
  443.7 10.2 %collective-permute-start.2 = (bf16[512,256]{1,0:T(8,128)(2,1)S(1)}, bf16[512,256]{1,0:T(8,128)(2,1)S(1)}, u32[]{:S(2)}, u32[]{:S(2)}) collective-permute-start(bf16[512,256]{1,0:T(8,128)(2,1)S(1)} %get-tuple-element.11), channel_id=1, source_target_pairs={{0,32},{32,0},{16,48},{48,16},{64,96},{96,64},{80,112},{112,80},{1... | collective-permute-start | bytes 786440 | tf_op jit(solution)/shard_map/ppermute | solution.py:19
  593.2 4.0 collective-permute-start.3
  598.3 15.9 %collective-permute-start.4 = (f32[512,256]{1,0:T(8,128)S(1)}, f32[512,256]{1,0:T(8,128)S(1)}, u32[]{:S(2)}, u32[]{:S(2)}) collective-permute-start(f32[512,256]{1,0:T(8,128)S(1)} %add.73), channel_id=1, source_target_pairs={{0,32},{32,0},{16,48},{48,16},{64,96},{96,64},{80,112},{112,80},{1... | collective-permute-start | bytes 1572872 | tf_op jit(solution)/shard_map/ppermute | solution.py:19
  614.3 10.9 %collective-permute-start.5 = (bf16[512,256]{1,0:T(8,128)(2,1)S(1)}, bf16[512,256]{1,0:T(8,128)(2,1)S(1)}, u32[]{:S(2)}, u32[]{:S(2)}) collective-permute-start(bf16[512,256]{1,0:T(8,128)(2,1)S(1)} %get-tuple-element.9), channel_id=1, source_target_pairs={{0,64},{64,0},{16,80},{80,16},{32,96},{96,32},{48,112},{112,48},{1... | collective-permute-start | bytes 786440 | tf_op jit(solution)/shard_map/ppermute | solution.py:19
Sparse Core Ops, SparseCore 0:
  156.9 136.8 all-reduce.3
  304.1 134.4 all-reduce.5
  458.8 134.3 all-reduce.7
